TPU v7x, 512 devices: a whole 4x8x8 slice. The times are simulated.
512 devices in a mesh: seq: 64 (over y, x, z_hi), tp: 8 (over z_lo, core).
Axes of the slice: x: 4, y: 8, z: 8 (z_hi: 2, z_lo: 4; z = z_hi * 4 + z_lo), core: 2. Of those that a mesh axis runs over, the one named last changes fastest.
Arguments:
- hidden_in: bfloat16 [16384, 2048], P('seq', 'tp'), may hold values from -6 to 6
- w_query: bfloat16 [2048, 2048], P(None, 'tp'), may hold values from -0.375 to 0.375
- w_keyval: bfloat16 [2048, 2, 2048], P(None, None, 'tp'), may hold values from -0.125 to 0.125
- w_out: bfloat16 [2048, 2048], P('tp'), may hold values from -0.125 to 0.125
- prompt_cache: bfloat16 [8192, 2, 2048], P('seq', None, 'tp'), may hold values from -160 to 160
- tail_cache: bfloat16 [128, 128, 2, 2048], P('seq', None, None, 'tp'), may hold values from -6 to 6
- tail_table: int32 [8, 16], replicated, may hold values from 0 to 127, as said below
- tail_len: int32 [8], replicated, may hold values from 1 to 2048
- shared_len: int32 [1], replicated, may hold values from 4096 to 8192
Outputs:
- hidden_out: bfloat16 [16384, 2048], P('seq', 'tp')
- new_cache: bfloat16 [16384, 2, 2048], P('seq', None, 'tp')
Inputs may be any that keep to these rules, and one draw needn't show every extreme that they name: Row r lists each of the slots r * 16 to (r + 1) * 16 - 1 once; block j of request r's tail is held in slot tail_table[r, j].
All inputs are finite; a program needn't handle non-finite values.
Results may differ from a plain program's by a relative error of at most 0.013.
Values may be sent and summed in bfloat16 or wider, within the bound.
A program may use at most 128 MiB of HBM per device.

v0:
```python
import jax
import jax.numpy as jnp
from jax import lax
from jax.sharding import PartitionSpec as P

HD = 128
REQ = 8
NEGATIVE = -1e30


def swapped(value, axis, stride):
    mask = 2**stride
    pairs = [(source, source ^ mask) for source in range(lax.axis_size(axis))]
    return lax.ppermute(value, axis, pairs)


def layer_norm(inputs):
    values = inputs.astype(jnp.float32)
    mean = jnp.mean(values, axis=-1, keepdims=True)
    centred = values - mean
    spread = jnp.mean(centred * centred, axis=-1, keepdims=True)
    return (centred * lax.rsqrt(spread + 1e-05)).astype(jnp.bfloat16)


def rotate(vectors, positions):
    half = vectors.shape[-1] // 2
    freqs = 10000.0 ** (-jnp.arange(half, dtype=jnp.float32) / half)
    angles = positions.astype(jnp.float32)[:, None, None] * freqs
    cosine = jnp.cos(angles)
    sine = jnp.sin(angles)
    first = vectors[..., :half]
    second = vectors[..., half:]
    return jnp.concatenate(
        [first * cosine - second * sine, second * cosine + first * sine], axis=-1
    )


def start_state(heads, queries, width):
    return (
        jnp.full((heads, queries), NEGATIVE, jnp.float32),
        jnp.zeros((heads, queries), jnp.float32),
        jnp.zeros((heads, queries, width), jnp.float32),
    )


def absorb(state, queries, keys, values, allowed):
    scores = jnp.einsum("hqd,khd->hqk", queries, keys, preferred_element_type=jnp.float32) * HD ** (
        -0.5
    )
    scores = jnp.where(allowed[None], scores, -jnp.inf)
    old_top, old_total, old_mixed = state
    new_top = jnp.maximum(old_top, jnp.max(scores, axis=2))
    factor = jnp.exp(old_top - new_top)
    weights = jnp.exp(scores - new_top[:, :, None])
    total = old_total * factor + jnp.sum(weights, axis=2)
    mixed = old_mixed * factor[:, :, None] + jnp.einsum(
        "hqk,khd->hqd", weights.astype(jnp.bfloat16), values, preferred_element_type=jnp.float32
    )
    return (new_top, total, mixed)


def combine(first, second):
    top = jnp.maximum(first[0], second[0])
    left = jnp.exp(first[0] - top)
    right = jnp.exp(second[0] - top)
    return (
        top,
        first[1] * left + second[1] * right,
        first[2] * left[:, :, None] + second[2] * right[:, :, None],
    )


def block_numbers(table_row, slot_ids):
    matches = table_row[None, :] == slot_ids[:, None]
    return jnp.sum(
        jnp.where(matches, jnp.arange(table_row.shape[0], dtype=jnp.int32)[None, :], 0), axis=1
    )


def local(
    hidden_in, w_query, w_keyval, w_out, prompt_cache, tail_cache, tail_table, tail_len, shared_len
):
    local_rows = hidden_in.shape[0]
    heads_here = w_query.shape[1] // HD
    group = lax.axis_size("seq") // REQ
    levels = group.bit_length() - 1
    seq_index = lax.axis_index("seq")
    request = seq_index // group
    member = seq_index % group
    offset = member * local_rows
    prompt_length = shared_len[0]
    own_length = lax.dynamic_index_in_dim(tail_len, request, 0, keepdims=False)
    table_row = lax.dynamic_index_in_dim(tail_table, request, 0, keepdims=False)
    slot_rows = tail_cache.shape[0]
    block_size = tail_cache.shape[1]
    whole = lax.all_gather(hidden_in, "tp", axis=1, tiled=True)
    normed = layer_norm(whole)
    query = jnp.dot(normed, w_query, preferred_element_type=jnp.float32).reshape(
        local_rows, heads_here, HD
    )
    projected = jnp.dot(
        normed, w_keyval.reshape(w_keyval.shape[0], -1), preferred_element_type=jnp.float32
    )
    projected = projected.reshape(local_rows, 2, heads_here, HD)
    positions = prompt_length + own_length + offset + jnp.arange(local_rows, dtype=jnp.int32)
    query = rotate(query, positions).astype(jnp.bfloat16)
    new_keys = rotate(projected[:, 0], positions).astype(jnp.bfloat16)
    new_values = projected[:, 1].astype(jnp.bfloat16)
    new_cache = jnp.stack(
        [new_keys.reshape(local_rows, -1), new_values.reshape(local_rows, -1)], axis=1
    )
    head_query = query.transpose(1, 0, 2)
    piece = lax.all_gather(prompt_cache, "seq", axis=0, tiled=True)
    length = piece.shape[0]
    allowed = (jnp.arange(length, dtype=jnp.int32) < prompt_length)[None, :]
    split = piece.reshape(length, 2, heads_here, HD)
    prompt_state = absorb(
        start_state(heads_here, local_rows, HD), head_query, split[:, 0], split[:, 1], allowed
    )
    packed = jnp.concatenate(
        [tail_cache.reshape(slot_rows * block_size, 2, tail_cache.shape[3]), new_cache], axis=0
    )
    per_member = packed.shape[0]
    for level in range(levels):
        other = swapped(packed, "seq", level)
        upper_half = seq_index // 2**level % 2 == 1
        packed = jnp.where(
            upper_half,
            jnp.concatenate([other, packed], axis=0),
            jnp.concatenate([packed, other], axis=0),
        )
    packed = packed.reshape(group, per_member, 2, heads_here, HD)
    tail_part = packed[:, : slot_rows * block_size].reshape(
        group * slot_rows * block_size, 2, heads_here, HD
    )
    fresh_part = packed[:, slot_rows * block_size :].reshape(group * local_rows, 2, heads_here, HD)
    slot_ids = request * group * slot_rows + jnp.arange(group * slot_rows, dtype=jnp.int32)
    tail_positions = (
        block_numbers(table_row, slot_ids)[:, None] * block_size
        + jnp.arange(block_size, dtype=jnp.int32)[None, :]
    ).reshape(-1)
    tail_allowed = (tail_positions < own_length)[None, :]
    fresh_allowed = (
        jnp.arange(group * local_rows, dtype=jnp.int32)[None, :]
        <= offset + jnp.arange(local_rows, dtype=jnp.int32)[:, None]
    )
    group_state = absorb(
        start_state(heads_here, local_rows, HD),
        head_query,
        tail_part[:, 0],
        tail_part[:, 1],
        tail_allowed,
    )
    group_state = absorb(group_state, head_query, fresh_part[:, 0], fresh_part[:, 1], fresh_allowed)
    final = combine(prompt_state, group_state)
    attended = (
        (final[2] / final[1][:, :, None])
        .astype(jnp.bfloat16)
        .transpose(1, 0, 2)
        .reshape(local_rows, -1)
    )
    summed = lax.psum_scatter(
        lax.dot_general(
            w_out, attended, (((0,), (1,)), ((), ())), preferred_element_type=jnp.float32
        ).astype(jnp.bfloat16),
        "tp",
        scatter_dimension=0,
        tiled=True,
    ).astype(jnp.float32)
    hidden_out = (hidden_in.astype(jnp.float32) + summed.T).astype(jnp.bfloat16)
    return (hidden_out, new_cache)


def solution(mesh):
    return jax.shard_map(
        local,
        mesh=mesh,
        in_specs=(
            P("seq", "tp"),
            P(None, "tp"),
            P(None, None, "tp"),
            P("tp", None),
            P("seq", None, "tp"),
            P("seq", None, None, "tp"),
            P(),
            P(),
            P(),
        ),
        out_specs=(P("seq", "tp"), P("seq", None, "tp")),
        check_vma=False,
    )
```

profile of v0, /device:TPU:12, one launch (start us, length us, event | category | flops | bytes accessed | tf_op | source)
XLA Modules:
  0.0 378.5 jit_solution(9868190781230296545)
XLA Ops:
  7.2 0.0 copy-start
  7.2 0.0 all-gather.3.cloned.1.call-start
  7.2 0.7 all-gather.3.cloned.1.call-update
  7.9 0.0 all-gather.5.cloned.1.call-start
  8.0 1.7 copy.36
  9.6 0.0 all-gather.5.cloned.1.call-update
  9.7 0.0 reduce-scatter.2.cloned.1.call-start
  10.4 1.1 copy.50
  11.5 0.0 copy-start.17
  11.5 2.0 copy.57
  13.5 2.4 copy.39
  16.0 0.0 copy-done.17
  16.0 0.7 dynamic_slice.8
  17.4 0.5 multiply_cosine_fusion
  17.9 32.5 %all-gather.3.cloned.1.call-done = bf16[256,2048]{1,0:T(8,128)(2,1)} async-done(((bf16[256,256]{1,0:T(8,128)(2,1)}), bf16[256,2048]{1,0:T(8,128)(2,1)}) %all-gather.3.cloned.1.call-update) | async-done | bytes 1048592 | tf_op jit(solution)/shard_map/all_gather | solution.py:96
  50.4 1.6 convert_reduce_fusion
  52.0 1.6 fusion.16
  53.6 2.8 fusion.62
  56.5 0.7 fusion.85
  57.2 0.1 copy.52
  57.3 0.1 copy.51
  57.5 0.1 copy.54
  57.6 0.9 subtract_convert_fusion.1
  58.5 0.1 pad_maximum_fusion.1
  58.6 0.1 copy.41
  58.8 5.4 %collective-permute-start = (bf16[512,2,256]{0,2,1:T(8,128)(2,1)S(1)}, bf16[512,2,256]{0,2,1:T(8,128)(2,1)S(1)}, u32[]{:S(2)}, u32[]{:S(2)}) collective-permute-start(bf16[512,2,256]{0,2,1:T(8,128)(2,1)S(1)} %maximum_maximum_fusion), channel_id=1, source_target_pairs={{0,8},{8,0},{16,24},{24,16},{32,40},{40,32},{48,56},{56,48},{64,72... | collective-permute-start | bytes 1572872 | tf_op jit(solution)/shard_map/ppermute | solution.py:14
  64.2 25.7 %collective-permute-done = bf16[512,2,256]{0,2,1:T(8,128)(2,1)S(1)} collective-permute-done((bf16[512,2,256]{0,2,1:T(8,128)(2,1)S(1)}, bf16[512,2,256]{0,2,1:T(8,128)(2,1)S(1)}, u32[]{:S(2)}, u32[]{:S(2)}) %collective-permute-start) | collective-permute-done | bytes 524320 | tf_op jit(solution)/shard_map/ppermute | solution.py:14
  89.9 0.3 maximum_select_fusion.2
  90.2 3.1 collective-permute-start.1
  93.3 23.2 %collective-permute-done.1 = bf16[1024,2,256]{0,2,1:T(8,128)(2,1)} collective-permute-done((bf16[1024,2,256]{0,2,1:T(8,128)(2,1)S(1)}, bf16[1024,2,256]{0,2,1:T(8,128)(2,1)}, u32[]{:S(2)}, u32[]{:S(2)}) %collective-permute-start.1) | collective-permute-done | bytes 1048608 | tf_op jit(solution)/shard_map/ppermute | solution.py:14
  116.5 3.0 maximum_select_fusion.1
  119.5 2.7 collective-permute-start.2
  122.2 0.7 dynamic-slice_bitcast_fusion
  122.9 0.2 select_reduce_fusion
  123.1 0.8 fusion.65
  123.9 1.2 iota_compare_fusion
  125.1 43.9 %collective-permute-done.2 = bf16[2048,2,256]{0,2,1:T(8,128)(2,1)} collective-permute-done((bf16[2048,2,256]{0,2,1:T(8,128)(2,1)S(1)}, bf16[2048,2,256]{0,2,1:T(8,128)(2,1)}, u32[]{:S(2)}, u32[]{:S(2)}) %collective-permute-start.2) | collective-permute-done | bytes 2097184 | tf_op jit(solution)/shard_map/ppermute | solution.py:14
  169.0 3.7 maximum_select_fusion
  172.7 2.2 copy.58
  174.9 1.7 fusion.87
  176.6 4.6 %copy.56 = bf16[8,256,2,2,128]{4,1,0,3,2:T(8,128)(2,1)} copy(bf16[8,256,2,2,128]{1,0,4,3,2:T(8,128)(2,1)} %get-tuple-element.6) | data formatting | bytes 4194304
  181.2 2.9 copy.55
  184.1 2.2 fusion.7
  186.4 1.2 fusion.8
  187.6 0.7 copy-done.1
  188.3 1.3 copy-done.4
  189.6 2.0 fusion.9
  191.6 104.3 %all-gather.5.cloned.1.call-done = bf16[8192,2,256]{0,2,1:T(8,128)(2,1)} async-done(((bf16[128,2,256]{0,2,1:T(8,128)(2,1)}), bf16[8192,2,256]{0,2,1:T(8,128)(2,1)}) %all-gather.5.cloned.1.call-update) | async-done | bytes 8388624 | tf_op jit(solution)/shard_map/all_gather | solution.py:113
  295.9 9.6 %fusion = (f32[2,256]{1,0:T(2,128)S(1)}, f32[2,256,8192]{2,1,0:T(8,128)}) fusion(pred[8192]{0:T(1024)(128)(4,1)S(1)} %iota_compare_fusion.1, bf16[8192,2,2,128]{0,3,2,1:T(8,128)(2,1)} %bitcast.195, bf16[256,2,64]{2,0,1:T(8,128)(2,1)S(1)} %copy-done.14, bf16[256,2,64]{2,0,1:T(8,128)(2,1)S(1)} %copy-done.13), kind=kOutput, calls=%fused_computation.2 | convolution fusion | flops 1086586368 | bytes 21112832 | tf_op jit(solution)/shard_map/hqd,khd->hqk/dot_general | solution.py:47
  305.5 9.9 %fusion.1 = f32[2,256]{1,0:T(2,128)S(1)} fusion(f32[2,256,8192]{2,1,0:T(8,128)} %get-tuple-element.31, f32[2,256]{1,0:T(2,128)S(1)} %broadcast_maximum_fusion.1, pred[8192]{0:T(1024)(128)(4,1)S(1)} %iota_compare_fusion.1), kind=kLoop, calls=%fused_computation.3 | loop fusion | flops 16776704 | bytes 16789504 | tf_op jit(solution)/shard_map/reduce_sum | solution.py:55
  315.5 0.0 copy-start.9
  315.5 0.0 copy-done.2
  315.5 3.5 fusion.51
  319.1 0.0 copy-done.5
  319.1 0.5 copy-done.9
  319.6 1.3 fusion.45
  320.9 2.1 copy-done.10
  323.0 7.8 %fusion.57 = bf16[256,2,128]{0,2,1:T(8,128)(2,1)S(1)} fusion(f32[256,2,128]{0,2,1:T(8,128)S(1)} %fusion.45, bf16[8192,2,2,128]{0,3,2,1:T(8,128)(2,1)S(1)} %bitcast.196, f32[2,256,8192]{2,1,0:T(8,128)} %get-tuple-element.31, f32[2,256]{1,0:T(2,128)S(1)} %broadcast_maximum_fusion.1, pred[8192]{0:T(1024)(128)(4,1)S(1)} %iota_compare_fusion.1, ...), kind=kOutput, calls=%fused_computation.46 | convolution fusion | flops 1090846720 | bytes 21381120 | tf_op jit(solution)/shard_map/hqk,khd->hqd/dot_general | solution.py:56
  330.8 0.0 copy-start.15
  330.8 1.4 fusion.15
  332.3 0.0 reduce-scatter.2.cloned.1.call-update
  332.3 0.9 copy.46
  333.2 37.2 %reduce-scatter.2.cloned.1.call-done = bf16[256,256]{0,1:T(8,128)(2,1)} async-done(((bf16[2048,256]{0,1:T(8,128)(2,1)}), bf16[256,256]{0,1:T(8,128)(2,1)}) %reduce-scatter.2.cloned.1.call-update) | async-done | bytes 131088 | tf_op jit(solution)/shard_map/reduce_scatter | solution.py:162
  370.4 1.6 fusion.64
  (41 shorter events, 0.3 us)
Async XLA Ops:
  7.2 323.7 %copy-start = (bf16[256,2048]{1,0:T(8,128)(2,1)S(1)}, bf16[256,2048]{1,0:T(8,128)(2,1)}, u32[]{:S(2)}) copy-start(bf16[256,2048]{1,0:T(8,128)(2,1)} %param.12) | copy-start | bytes 3145732
  7.2 43.2 %all-gather.3.cloned.1.call-start = ((), (), s32[]{:S(2)}) async-start(), calls=%async_computation.1 | async-start | bytes 1179648 | tf_op jit(solution)/shard_map/all_gather | solution.py:96
  7.9 288.0 %all-gather.5.cloned.1.call-start = ((), (), s32[]{:S(2)}) async-start(), calls=%async_computation.2 | async-start | bytes 8519680 | tf_op jit(solution)/shard_map/all_gather | solution.py:113
  9.7 360.7 %reduce-scatter.2.cloned.1.call-start = ((), (), s32[]{:S(2)}) async-start(), calls=%async_computation.3 | async-start | bytes 1179648 | tf_op jit(solution)/shard_map/reduce_scatter | solution.py:162
  11.5 4.5 %copy-start.17 = (s32[8]{0:T(128)S(1)}, s32[8]{0:T(128)}, u32[]{:S(2)}) copy-start(s32[8]{0:T(128)} %param.16) | copy-start | bytes 100
  50.4 6.1 %copy-start.6 = (bf16[256,2048]{1,0:T(8,128)(2,1)S(1)}, bf16[256,2048]{1,0:T(8,128)(2,1)}, u32[]{:S(2)}) copy-start(bf16[256,2048]{1,0:T(8,128)(2,1)} %all-gather.3.cloned.1.call-done) | copy-start | bytes 3145732
  50.4 6.1 %copy-start.16 = (bf16[2048,256]{1,0:T(8,128)(2,1)S(1)}, bf16[2048,256]{1,0:T(8,128)(2,1)}, u32[]{:S(2)}) copy-start(bf16[2048,256]{1,0:T(8,128)(2,1)} %param.10) | copy-start | bytes 3145732
  58.7 34.6 %copy-start.11 = (bf16[256,2,128]{0,2,1:T(8,128)(2,1)}, bf16[256,2,128]{0,2,1:T(8,128)(2,1)S(1)}, u32[]{:S(2)}) copy-start(bf16[256,2,128]{0,2,1:T(8,128)(2,1)S(1)} %copy.41) | copy-start | bytes 393220
  58.8 31.1 %collective-permute-start = (bf16[512,2,256]{0,2,1:T(8,128)(2,1)S(1)}, bf16[512,2,256]{0,2,1:T(8,128)(2,1)S(1)}, u32[]{:S(2)}, u32[]{:S(2)}) collective-permute-start(bf16[512,2,256]{0,2,1:T(8,128)(2,1)S(1)} %maximum_maximum_fusion), channel_id=1, source_target_pairs={{0,8},{8,0},{16,24},{24,16},{32,40},{40,32},{48,56},{56,48},{64,72... | collective-permute-start | bytes 1572872 | tf_op jit(solution)/shard_map/ppermute | solution.py:14
  90.2 3.1 copy-start.3
  90.2 26.3 %collective-permute-start.1 = (bf16[1024,2,256]{0,2,1:T(8,128)(2,1)S(1)}, bf16[1024,2,256]{0,2,1:T(8,128)(2,1)}, u32[]{:S(2)}, u32[]{:S(2)}) collective-permute-start(bf16[1024,2,256]{0,2,1:T(8,128)(2,1)S(1)} %maximum_select_fusion.2), channel_id=1, source_target_pairs={{0,16},{8,24},{16,0},{24,8},{32,48},{40,56},{48,32},{56,40},{64,80... | collective-permute-start | bytes 3145736 | tf_op jit(solution)/shard_map/ppermute | solution.py:14
  119.5 49.4 %collective-permute-start.2 = (bf16[2048,2,256]{0,2,1:T(8,128)(2,1)S(1)}, bf16[2048,2,256]{0,2,1:T(8,128)(2,1)}, u32[]{:S(2)}, u32[]{:S(2)}) collective-permute-start(bf16[2048,2,256]{0,2,1:T(8,128)(2,1)S(1)} %maximum_select_fusion.1), channel_id=1, source_target_pairs={{0,32},{8,40},{16,48},{24,56},{32,0},{40,8},{48,16},{56,24},{64,96... | collective-permute-start | bytes 6291464 | tf_op jit(solution)/shard_map/ppermute | solution.py:14
  176.6 7.5 %copy-start.13 = (bf16[256,2,64]{2,0,1:T(8,128)(2,1)S(1)}, bf16[256,2,64]{2,0,1:T(8,128)(2,1)}, u32[]{:S(2)}) copy-start(bf16[256,2,64]{2,0,1:T(8,128)(2,1)} %get-tuple-element.8) | copy-start | bytes 196612
  176.6 7.5 %copy-start.14 = (bf16[256,2,64]{2,0,1:T(8,128)(2,1)S(1)}, bf16[256,2,64]{2,0,1:T(8,128)(2,1)}, u32[]{:S(2)}) copy-start(bf16[256,2,64]{2,0,1:T(8,128)(2,1)} %get-tuple-element.9) | copy-start | bytes 196612
  184.1 2.2 copy-start.7
  184.1 2.2 copy-start.8
  186.4 2.0 copy-start.1
  187.6 2.0 copy-start.4
  305.5 10.0 %copy-start.2 = (bf16[8,256,2,2,128]{4,1,0,3,2:T(8,128)(2,1)S(1)}, bf16[8,256,2,2,128]{4,1,0,3,2:T(8,128)(2,1)}, u32[]{:S(2)}) copy-start(bf16[8,256,2,2,128]{4,1,0,3,2:T(8,128)(2,1)} %copy.55) | copy-start | bytes 6291460
  315.5 3.6 copy-start.5
  315.5 4.1 %copy-start.9 = (bf16[8,256,2,2,128]{4,1,0,3,2:T(8,128)(2,1)S(1)}, bf16[8,256,2,2,128]{4,1,0,3,2:T(8,128)(2,1)}, u32[]{:S(2)}) copy-start(bf16[8,256,2,2,128]{4,1,0,3,2:T(8,128)(2,1)} %copy.56) | copy-start | bytes 6291460
  319.6 3.4 copy-start.10
  323.0 9.3 %copy-start.12 = (bf16[256,2,128]{0,2,1:T(8,128)(2,1)S(1)}, bf16[256,2,128]{0,2,1:T(8,128)(2,1)}, u32[]{:S(2)}) copy-start(bf16[256,2,128]{0,2,1:T(8,128)(2,1)} %copy-done.11) | copy-start | bytes 393220
  330.8 39.6 %copy-start.15 = (bf16[256,256]{1,0:T(8,128)(2,1)S(1)}, bf16[256,256]{1,0:T(8,128)(2,1)}, u32[]{:S(2)}) copy-start(bf16[256,256]{1,0:T(8,128)(2,1)} %param.9) | copy-start | bytes 393220
Sparse Core Ops, SparseCore 0:
  10.0 40.3 all-gather.2
  54.7 241.2 all-gather.4
  332.4 37.9 reduce-scatter.1
where the time goes:
time: 379 us; the launch traced here: 378 us
  waiting for transfers between devices  267 us (70%)
  matrix products  30.5 us (8%)
  other arithmetic  27.6 us (7%)
  local copies, waits for them, and re-layouts  26.1 us (7%)
  between operations  15.6 us (4%)
  starting transfers between devices  11.3 us (3%)
    all_gather x1, waiting for transfers between devices, local(): piece = lax.all_gather(prompt_cache, 'seq', axis=0, tiled=True)  104 us
    ppermute x3, waiting for transfers between devices, swapped(): return lax.ppermute(value, axis, pairs)  92.8 us
    reduce_scatter x1, waiting for transfers between devices, local(): lax.psum_scatter(lax.dot_general(w_out, attended, (((0,), (1,)), ((), ())...  37.2 us
    all_gather x1, waiting for transfers between devices, local(): whole = lax.all_gather(hidden_in, 'tp', axis=1, tiled=True)  32.5 us
    unnamed x45, local copies, waits for them, and re-layouts  19.4 us
    dot_general x3, matrix products, absorb(): jnp.einsum('hqd,khd->hqk', queries, keys, preferred_element_type=jnp.floa...  13 us
    dot_general x3, matrix products, absorb(): jnp.einsum('hqk,khd->hqd', weights.astype(jnp.bfloat16), values, preferre...  12.6 us
    reduce_sum x2, other arithmetic, absorb(): total = old_total * factor + jnp.sum(weights, axis=2)  12 us
  transfers between devices with their start and end apart: 6, of which 6 were waited for; matrix products, arithmetic and copies ran while one was open for 12% of the time, Pallas kernels for 0%

commit v1 on v0

--- a/solution.py
+++ b/solution.py
@@ -1,3 +1,4 @@
+import functools
 import jax
 import jax.numpy as jnp
 from jax import lax
@@ -6,6 +7,17 @@
 HD = 128
 REQ = 8
 NEGATIVE = -1e30
+
+
+def sides_view(block_in, dev_axis):
+    z2 = lax.axis_size(dev_axis)
+    r1 = jnp.stack(z2 * [block_in], 0)
+    arr_now = lax.all_to_all(r1, axis_name=dev_axis, split_axis=0, concat_axis=0)
+    view_out = jnp.concatenate(arr_now, 0)
+    return view_out
+
+
+direct_tasks = functools.partial(sides_view, dev_axis="seq")
 
 
 def swapped(value, axis, stride):
@@ -110,7 +122,7 @@
         [new_keys.reshape(local_rows, -1), new_values.reshape(local_rows, -1)], axis=1
     )
     head_query = query.transpose(1, 0, 2)
-    piece = lax.all_gather(prompt_cache, "seq", axis=0, tiled=True)
+    piece = direct_tasks(prompt_cache)
     length = piece.shape[0]
     allowed = (jnp.arange(length, dtype=jnp.int32) < prompt_length)[None, :]
     split = piece.reshape(length, 2, heads_here, HD)

time: 379 us -> 498 us (1.31)
  the two profiles are of different devices: /device:TPU:12 before, /device:TPU:22 now
where the time goes in v1:
time: 498 us; the launch traced here: 497 us
  waiting for transfers between devices  343 us (69%)
  local copies, waits for them, and re-layouts  54.5 us (11%)
  matrix products  30.5 us (6%)
  other arithmetic  27.8 us (6%)
  starting transfers between devices  25.2 us (5%)
  between operations  15.9 us (3%)
    all_gather x1, waiting for transfers between devices, local(): whole = lax.all_gather(hidden_in, 'tp', axis=1, tiled=True)  197 us
    ppermute x3, waiting for transfers between devices, swapped(): return lax.ppermute(value, axis, pairs)  92.9 us
    reduce_scatter x1, waiting for transfers between devices, local(): lax.psum_scatter(lax.dot_general(w_out, attended, (((0,), (1,)), ((), ())...  52.6 us
    all_to_all x1, starting transfers between devices, sides_view(): lax.all_to_all(r1, axis_name=dev_axis, split_axis=0, concat_axis=0)  19.2 us
    unnamed x49, local copies, waits for them, and re-layouts  18.1 us
    another operation x1, local copies, waits for them, and re-layouts, local(): split = piece.reshape(length, 2, heads_here, HD)  13.3 us
    dot_general x3, matrix products, absorb(): jnp.einsum('hqd,khd->hqk', queries, keys, preferred_element_type=jnp.floa...  13 us
    dot_general x3, matrix products, absorb(): jnp.einsum('hqk,khd->hqd', weights.astype(jnp.bfloat16), values, preferre...  12.6 us
  transfers between devices with their start and end apart: 6, of which 5 were waited for; matrix products, arithmetic and copies ran while one was open for 8% of the time, Pallas kernels for 0%

profile of v1, /device:TPU:22, one launch (start us, length us, event | category | flops | bytes accessed | tf_op | source)
XLA Modules:
  0.0 496.9 jit_solution(15081072633934950834)
XLA Ops:
  7.2 0.0 copy-start
  7.2 1.1 copy.50
  8.3 5.3 %stack.4 = bf16[64,128,2,256]{1,3,2,0:T(8,128)(2,1)} broadcast(bf16[128,2,256]{0,2,1:T(8,128)(2,1)S(1)} %copy.50), dimensions={1,2,3} | broadcast | bytes 8519680 | tf_op jit(solution)/shard_map/stack | solution.py:14
  13.6 19.2 %all-to-all-start = ((bf16[64,128,2,256]{1,3,2,0:T(8,128)(2,1)}), bf16[64,128,2,256]{1,3,2,0:T(8,128)(2,1)}, u32[]{:S(2)}, u32[]{:S(2)}) async-start(bf16[64,128,2,256]{1,3,2,0:T(8,128)(2,1)} %stack.4), calls=%async_computation | async-start | bytes 16777216 | tf_op jit(solution)/shard_map/all_to_all | solution.py:15
  32.8 0.0 all-gather.2.cloned.1.call-start
  32.8 0.7 all-gather.2.cloned.1.call-update
  33.5 0.0 reduce-scatter.2.cloned.1.call-start
  34.3 0.2 copy.65
  34.4 0.0 copy-start.17
  34.5 2.0 copy.72
  36.5 2.5 copy.54
  39.0 0.6 dynamic_slice.8
  40.2 0.5 multiply_cosine_fusion
  40.8 196.8 %all-gather.2.cloned.1.call-done = bf16[256,2048]{1,0:T(8,128)(2,1)} async-done(((bf16[256,256]{1,0:T(8,128)(2,1)}), bf16[256,2048]{1,0:T(8,128)(2,1)}) %all-gather.2.cloned.1.call-update) | async-done | bytes 1048592 | tf_op jit(solution)/shard_map/all_gather | solution.py:108
  237.6 1.6 convert_reduce_fusion
  239.2 1.6 fusion.16
  240.9 2.7 fusion.62
  243.7 0.7 fusion.85
  244.4 0.1 copy.67
  244.6 0.1 copy.66
  244.7 0.1 copy.69
  244.8 0.9 subtract_convert_fusion.1
  245.7 0.1 pad_maximum_fusion.1
  245.8 0.1 copy.56
  246.0 1.9 collective-permute-start
  247.9 27.7 %collective-permute-done = bf16[512,2,256]{0,2,1:T(8,128)(2,1)S(1)} collective-permute-done((bf16[512,2,256]{0,2,1:T(8,128)(2,1)S(1)}, bf16[512,2,256]{0,2,1:T(8,128)(2,1)S(1)}, u32[]{:S(2)}, u32[]{:S(2)}) %collective-permute-start) | collective-permute-done | bytes 524320 | tf_op jit(solution)/shard_map/ppermute | solution.py:26
  275.7 0.3 maximum_select_fusion.2
  276.0 1.9 collective-permute-start.1
  278.0 22.1 %collective-permute-done.1 = bf16[1024,2,256]{0,2,1:T(8,128)(2,1)} collective-permute-done((bf16[1024,2,256]{0,2,1:T(8,128)(2,1)S(1)}, bf16[1024,2,256]{0,2,1:T(8,128)(2,1)}, u32[]{:S(2)}, u32[]{:S(2)}) %collective-permute-start.1) | collective-permute-done | bytes 1048608 | tf_op jit(solution)/shard_map/ppermute | solution.py:26
  300.0 3.0 maximum_select_fusion.1
  303.0 2.1 collective-permute-start.2
  305.2 0.7 dynamic-slice_bitcast_fusion
  305.9 0.2 select_reduce_fusion
  306.1 0.7 fusion.65
  306.8 1.2 iota_compare_fusion
  308.0 43.1 %collective-permute-done.2 = bf16[2048,2,256]{0,2,1:T(8,128)(2,1)} collective-permute-done((bf16[2048,2,256]{0,2,1:T(8,128)(2,1)S(1)}, bf16[2048,2,256]{0,2,1:T(8,128)(2,1)}, u32[]{:S(2)}, u32[]{:S(2)}) %collective-permute-start.2) | collective-permute-done | bytes 2097184 | tf_op jit(solution)/shard_map/ppermute | solution.py:26
  351.0 3.8 maximum_select_fusion
  354.8 2.2 copy.73
  357.1 1.6 fusion.87
  358.7 4.5 copy.71
  363.2 2.9 copy.70
  366.2 0.0 copy-done.12
  366.2 2.2 fusion.7
  368.4 1.2 fusion.8
  369.6 0.8 copy-done.1
  370.4 1.3 copy-done.4
  371.7 2.2 fusion.9
  373.9 0.0 all-to-all-done
  373.9 12.0 %copy.51 = bf16[64,128,2,256]{1,0,3,2:T(8,128)(2,1)} copy(bf16[64,128,2,256]{1,3,2,0:T(8,128)(2,1)} %all-to-all-done) | data formatting | bytes 16777216 | tf_op jit(solution)/shard_map/all_to_all | solution.py:15
  385.9 13.3 %reshape_reshape.3 = bf16[8192,2,2,128]{0,3,2,1:T(8,128)(2,1)} reshape(bf16[64,128,2,256]{1,0,3,2:T(8,128)(2,1)} %copy.51) | data formatting | bytes 16777216 | tf_op jit(solution)/shard_map/reshape;reshape | solution.py:128
  399.2 9.6 %fusion = (f32[2,256]{1,0:T(2,128)S(1)}, f32[2,256,8192]{2,1,0:T(8,128)}) fusion(pred[8192]{0:T(1024)(128)(4,1)S(1)} %iota_compare_fusion.1, bf16[8192,2,2,128]{0,3,2,1:T(8,128)(2,1)} %reshape_reshape.3, bf16[256,2,64]{2,0,1:T(8,128)(2,1)S(1)} %copy-done.13, bf16[256,2,64]{2,0,1:T(8,128)(2,1)S(1)} %copy-done.12), kind=kOutput, calls=%fused_computation.2 | convolution fusion | flops 1086586368 | bytes 21112832 | tf_op jit(solution)/shard_map/hqd,khd->hqk/dot_general | solution.py:59
  408.8 9.9 %fusion.1 = f32[2,256]{1,0:T(2,128)S(1)} fusion(f32[2,256,8192]{2,1,0:T(8,128)} %get-tuple-element.33, f32[2,256]{1,0:T(2,128)S(1)} %broadcast_maximum_fusion.1, pred[8192]{0:T(1024)(128)(4,1)S(1)} %iota_compare_fusion.1), kind=kLoop, calls=%fused_computation.3 | loop fusion | flops 16776704 | bytes 16789504 | tf_op jit(solution)/shard_map/reduce_sum | solution.py:67
  418.8 0.0 slice-start
  418.8 3.5 fusion.51
  422.4 0.5 copy-done.9
  422.9 1.3 fusion.45
  424.2 1.4 slice-done.1
  425.6 7.8 %fusion.57 = bf16[256,2,128]{0,2,1:T(8,128)(2,1)S(1)} fusion(f32[256,2,128]{0,2,1:T(8,128)S(1)} %fusion.45, bf16[8192,2,2,128]{0,3,2,1:T(8,128)(2,1)S(1)} %bitcast.189, f32[2,256,8192]{2,1,0:T(8,128)} %get-tuple-element.33, f32[2,256]{1,0:T(2,128)S(1)} %broadcast_maximum_fusion.1, pred[8192]{0:T(1024)(128)(4,1)S(1)} %iota_compare_fusion.1, ...), kind=kOutput, calls=%fused_computation.46 | convolution fusion | flops 1090846720 | bytes 21381120 | tf_op jit(solution)/shard_map/hqk,khd->hqd/dot_general | solution.py:68
  433.4 0.0 copy-start.14
  433.5 1.4 fusion.15
  434.9 0.0 reduce-scatter.2.cloned.1.call-update
  435.0 0.9 copy.61
  435.8 52.6 %reduce-scatter.2.cloned.1.call-done = bf16[256,256]{0,1:T(8,128)(2,1)} async-done(((bf16[2048,256]{0,1:T(8,128)(2,1)}), bf16[256,256]{0,1:T(8,128)(2,1)}) %reduce-scatter.2.cloned.1.call-update) | async-done | bytes 131088 | tf_op jit(solution)/shard_map/reduce_scatter | solution.py:174
  488.4 1.6 fusion.64
  (48 shorter events, 0.3 us)
Async XLA Ops:
  7.2 426.3 %copy-start = (bf16[256,2048]{1,0:T(8,128)(2,1)S(1)}, bf16[256,2048]{1,0:T(8,128)(2,1)}, u32[]{:S(2)}) copy-start(bf16[256,2048]{1,0:T(8,128)(2,1)} %param.12) | copy-start | bytes 3145732
  13.6 20.6 %copy-start.15 = (bf16[2,128,2,256]{3,2,1,0:T(2,128)(2,1)S(1)}, bf16[2,128,2,256]{3,2,1,0:T(2,128)(2,1)}, u32[]{:S(2)}) copy-start(bf16[2,128,2,256]{3,2,1,0:T(2,128)(2,1)} %param.14) | copy-start | bytes 786436
  13.6 360.3 %all-to-all-start = ((bf16[64,128,2,256]{1,3,2,0:T(8,128)(2,1)}), bf16[64,128,2,256]{1,3,2,0:T(8,128)(2,1)}, u32[]{:S(2)}, u32[]{:S(2)}) async-start(bf16[64,128,2,256]{1,3,2,0:T(8,128)(2,1)} %stack.4), calls=%async_computation | async-start | bytes 16777216 | tf_op jit(solution)/shard_map/all_to_all | solution.py:15
  32.8 204.8 %all-gather.2.cloned.1.call-start = ((), (), s32[]{:S(2)}) async-start(), calls=%async_computation.2 | async-start | bytes 1179648 | tf_op jit(solution)/shard_map/all_gather | solution.py:108
  33.5 454.9 %reduce-scatter.2.cloned.1.call-start = ((), (), s32[]{:S(2)}) async-start(), calls=%async_computation.3 | async-start | bytes 1179648 | tf_op jit(solution)/shard_map/reduce_scatter | solution.py:174
  34.4 4.5 copy-start.17
  237.6 6.1 %copy-start.6 = (bf16[256,2048]{1,0:T(8,128)(2,1)S(1)}, bf16[256,2048]{1,0:T(8,128)(2,1)}, u32[]{:S(2)}) copy-start(bf16[256,2048]{1,0:T(8,128)(2,1)} %all-gather.2.cloned.1.call-done) | copy-start | bytes 3145732
  237.6 6.1 %copy-start.16 = (bf16[2048,256]{1,0:T(8,128)(2,1)S(1)}, bf16[2048,256]{1,0:T(8,128)(2,1)}, u32[]{:S(2)}) copy-start(bf16[2048,256]{1,0:T(8,128)(2,1)} %param.10) | copy-start | bytes 3145732
  245.9 32.0 %copy-start.10 = (bf16[256,2,128]{0,2,1:T(8,128)(2,1)}, bf16[256,2,128]{0,2,1:T(8,128)(2,1)S(1)}, u32[]{:S(2)}) copy-start(bf16[256,2,128]{0,2,1:T(8,128)(2,1)S(1)} %copy.56) | copy-start | bytes 393220
  246.0 29.7 %collective-permute-start = (bf16[512,2,256]{0,2,1:T(8,128)(2,1)S(1)}, bf16[512,2,256]{0,2,1:T(8,128)(2,1)S(1)}, u32[]{:S(2)}, u32[]{:S(2)}) collective-permute-start(bf16[512,2,256]{0,2,1:T(8,128)(2,1)S(1)} %maximum_maximum_fusion), channel_id=1, source_target_pairs={{0,8},{8,0},{16,24},{24,16},{32,40},{40,32},{48,56},{56,48},{64,72... | collective-permute-start | bytes 1572872 | tf_op jit(solution)/shard_map/ppermute | solution.py:26
  276.0 2.0 copy-start.3
  276.0 24.0 %collective-permute-start.1 = (bf16[1024,2,256]{0,2,1:T(8,128)(2,1)S(1)}, bf16[1024,2,256]{0,2,1:T(8,128)(2,1)}, u32[]{:S(2)}, u32[]{:S(2)}) collective-permute-start(bf16[1024,2,256]{0,2,1:T(8,128)(2,1)S(1)} %maximum_select_fusion.2), channel_id=1, source_target_pairs={{0,16},{8,24},{16,0},{24,8},{32,48},{40,56},{48,32},{56,40},{64,80... | collective-permute-start | bytes 3145736 | tf_op jit(solution)/shard_map/ppermute | solution.py:26
  303.0 48.0 %collective-permute-start.2 = (bf16[2048,2,256]{0,2,1:T(8,128)(2,1)S(1)}, bf16[2048,2,256]{0,2,1:T(8,128)(2,1)}, u32[]{:S(2)}, u32[]{:S(2)}) collective-permute-start(bf16[2048,2,256]{0,2,1:T(8,128)(2,1)S(1)} %maximum_select_fusion.1), channel_id=1, source_target_pairs={{0,32},{8,40},{16,48},{24,56},{32,0},{40,8},{48,16},{56,24},{64,96... | collective-permute-start | bytes 6291464 | tf_op jit(solution)/shard_map/ppermute | solution.py:26
  358.7 7.5 %copy-start.12 = (bf16[256,2,64]{2,0,1:T(8,128)(2,1)S(1)}, bf16[256,2,64]{2,0,1:T(8,128)(2,1)}, u32[]{:S(2)}) copy-start(bf16[256,2,64]{2,0,1:T(8,128)(2,1)} %get-tuple-element.10) | copy-start | bytes 196612
  358.7 7.5 %copy-start.13 = (bf16[256,2,64]{2,0,1:T(8,128)(2,1)S(1)}, bf16[256,2,64]{2,0,1:T(8,128)(2,1)}, u32[]{:S(2)}) copy-start(bf16[256,2,64]{2,0,1:T(8,128)(2,1)} %get-tuple-element.11) | copy-start | bytes 196612
  366.2 2.2 copy-start.7
  366.2 2.3 copy-start.8
  368.4 2.0 copy-start.1
  369.6 2.0 copy-start.4
  408.8 10.0 %copy-start.2 = (bf16[8,256,2,2,128]{4,1,0,3,2:T(8,128)(2,1)S(1)}, bf16[8,256,2,2,128]{4,1,0,3,2:T(8,128)(2,1)}, u32[]{:S(2)}) copy-start(bf16[8,256,2,2,128]{4,1,0,3,2:T(8,128)(2,1)} %copy.70) | copy-start | bytes 6291460
  418.8 3.6 copy-start.5
  418.8 4.1 copy-start.9
  418.8 5.4 %slice-start = ((s8[8388608]{0:T(1024)(128)(4,1)}), s8[4194304]{0:T(1024)(128)(4,1)S(1)}, s32[]{:S(2)}) async-start(s8[8388608]{0:T(1024)(128)(4,1)} %bitcast.188), calls=%async_computation.4 | async-start | bytes 8388608
  422.9 2.7 slice-start.1
  425.6 9.3 %copy-start.11 = (bf16[256,2,128]{0,2,1:T(8,128)(2,1)S(1)}, bf16[256,2,128]{0,2,1:T(8,128)(2,1)}, u32[]{:S(2)}) copy-start(bf16[256,2,128]{0,2,1:T(8,128)(2,1)} %copy-done.10) | copy-start | bytes 393220
  433.4 55.0 %copy-start.14 = (bf16[256,256]{1,0:T(8,128)(2,1)S(1)}, bf16[256,256]{1,0:T(8,128)(2,1)}, u32[]{:S(2)}) copy-start(bf16[256,256]{1,0:T(8,128)(2,1)} %param.9) | copy-start | bytes 393220
Sparse Core Ops, SparseCore 0:
  35.6 201.9 all-gather.1
  435.0 53.3 reduce-scatter.1
